TPU v7x, 768 devices: a whole 4x8x12 slice. The times are simulated.
768 devices in a mesh: dp: 16 (over y, core), section: 48 (over x, z).
Axes of the slice: x: 4, y: 8, z: 12, core: 2. Of those that a mesh axis runs over, the one named last changes fastest.
Arguments:
- lat_raw: bfloat16 [48, 16, 16, 16], P('section', None, 'dp'), may hold values from -6 to 6
- txt_raw: bfloat16 [48, 16, 16, 4096], P('section', None, 'dp'), may hold values from -6 to 6
- lat_embed: bfloat16 [16, 1024], replicated, may hold values from -1.5 to 1.5
- txt_embed: bfloat16 [4096, 1024], replicated, may hold values from -0.09375 to 0.09375
- image_owner: int32 [48, 16], replicated, may hold values from 0 to 15, each once within a row
- text_len: int32 [48, 16], replicated, may hold values from 1 to 16
- weights: bfloat16 [48, 1024, 1024], P('section', 'dp'), may hold values from -0.1875 to 0.1875
- top_grad: bfloat16 [16, 48, 32, 1024], P('dp', 'section'), may hold values from -0.75 to 0.75
Outputs:
- weight_grads: float32 [48, 1024, 1024], P('section', 'dp')
Inputs may be any that keep to these rules, and one draw needn't show every extreme that they name: `image_owner`: each row names every data shard exactly once.
All inputs are finite; a program needn't handle non-finite values.
Results may differ from a plain program's by a relative error of at most 0.023.
Values may be sent and summed in bfloat16 or wider, within the bound.
A program may use at most 32 MiB of HBM per device.

v0:
```python
import jax
import jax.numpy as jnp
from jax import lax
from jax.sharding import PartitionSpec as P

LAT = 16
PIPE = 8


norm_eps = 1e-06


def extended(cells, sides, width):
    for axis, dim in sides:
        count = lax.axis_size(axis)
        ends = count - 1
        head = lax.slice_in_dim(cells, 0, width, axis=dim)
        tail = lax.slice_in_dim(cells, cells.shape[dim] - width, cells.shape[dim], axis=dim)
        cells = jnp.concatenate(
            [
                lax.ppermute(tail, axis, [(i, (i + 1) % count) for i in range(ends)]),
                cells,
                lax.ppermute(head, axis, [((i + 1) % count, i) for i in range(ends)]),
            ],
            axis=dim,
        )
    return cells


def modulate(tokens_in, text_mask, text_count):
    inv_norm = lax.rsqrt(jnp.mean(tokens_in * tokens_in, axis=1, keepdims=True) + norm_eps)
    normed = tokens_in * inv_norm
    pooled = 0.5 * jnp.sum(normed * text_mask[:, None], axis=0) / text_count
    return normed * (1.0 + pooled)[None, :]


def silu_slope(gate_preactivation):
    sigmoid_v = jax.nn.sigmoid(gate_preactivation)
    return sigmoid_v * (1.0 + gate_preactivation * (1.0 - sigmoid_v))


def neighbours(down_slot, up_slot):
    padded = extended(jnp.stack([down_slot, up_slot]), (("section", 0),), 1)
    return (padded[3], padded[0])


def local(lat_raw, txt_raw, lat_embed, txt_embed, image_owner, text_len, weights, top_grad):
    my_shard = lax.axis_index("dp")
    section_here = lax.axis_index("section")
    section_pos = section_here % PIPE
    first_col = section_here - section_pos
    senders = jnp.argsort(image_owner, axis=1, stable=True)
    dest_order = lax.dynamic_index_in_dim(senders, section_here, 0, keepdims=False)
    text_rows = jnp.einsum(
        "jrc,cf->jrf", txt_raw[0], txt_embed, preferred_element_type=jnp.float32
    ).astype(jnp.bfloat16)
    lat_enc = jnp.einsum(
        "jrc,cf->jrf", lat_raw[0], lat_embed, preferred_element_type=jnp.float32
    ).astype(jnp.bfloat16)
    lat_payload = jnp.take(lat_enc, dest_order, axis=0)
    got_lat, got_text = (
        lax.all_to_all(lat_payload, "dp", split_axis=0, concat_axis=0, tiled=True),
        lax.all_to_all(
            jnp.take(text_rows, dest_order, axis=0), "dp", split_axis=0, concat_axis=0, tiled=True
        ),
    )
    got_lat = got_lat.reshape(-1, got_lat.shape[-1])
    feed_rows = jnp.concatenate([got_lat, got_text.reshape(-1, got_text.shape[-1])], axis=0)
    weight_part = weights[0]
    weight_fwd = lax.all_gather(weight_part, "dp", axis=0, tiled=True)
    lane_send = lax.dynamic_slice_in_dim(senders, first_col, PIPE, 0)
    lane_len = lax.dynamic_slice_in_dim(text_len, first_col, PIPE, 0)
    src_slots = lax.dynamic_index_in_dim(lane_send, my_shard, 1, keepdims=False)
    lane_lengths = jnp.take_along_axis(lane_len, src_slots[:, None], axis=1)[:, 0]
    positions = jnp.arange(feed_rows.shape[0])
    zero_rows = jnp.zeros_like(feed_rows)

    def mask_for(micro_idx):
        length = lax.dynamic_index_in_dim(
            lane_lengths, jnp.clip(micro_idx, 0, PIPE - 1), 0, keepdims=False
        )
        text_mask = ((positions >= LAT) & (positions < LAT + length)).astype(jnp.float32)
        return (text_mask, length.astype(jnp.float32))

    def forward(tokens_in, micro_idx):
        text_mask, text_count = mask_for(micro_idx)
        widened = tokens_in.astype(jnp.float32)
        hidden_layer_state = modulate(widened, text_mask, text_count).astype(jnp.bfloat16)
        gate_preactivation = jnp.dot(
            hidden_layer_state, weight_fwd, preferred_element_type=jnp.float32
        )
        return (widened + jax.nn.silu(gate_preactivation)).astype(jnp.bfloat16)

    def advance(turn_index, feed_slot, in_rows, stored):
        micro_idx = turn_index - section_pos
        active = (micro_idx >= 0) & (micro_idx < PIPE)
        tokens_in = jnp.where(section_pos == 0, feed_slot, in_rows)

        def advance_do_work(kept):
            placed = lax.dynamic_update_index_in_dim(
                kept, tokens_in, jnp.clip(micro_idx, 0, PIPE - 1), 0
            )
            return (forward(tokens_in, micro_idx), placed)

        def advance_no_work(kept):
            return (zero_rows, kept)

        return lax.cond(active, advance_do_work, advance_no_work, stored)

    final_turn = 2 * PIPE - 1
    stored = jnp.zeros((PIPE,) + feed_rows.shape, jnp.bfloat16)
    outbox, stored = advance(0, feed_rows, zero_rows, stored)

    def both_forward(turn_index, state_tuple):
        feed_slot, outbox, stored = state_tuple
        feed_slot, in_rows = neighbours(feed_slot, outbox)
        outbox, stored = advance(turn_index, feed_slot, in_rows, stored)
        return (feed_slot, outbox, stored)

    state_tuple = lax.fori_loop(1, final_turn, both_forward, (feed_rows, outbox, stored))
    stored = state_tuple[2]

    def backward(tokens_in, grad_rows, micro_idx):
        text_mask, text_count = mask_for(micro_idx)
        widened = tokens_in.astype(jnp.float32)
        hidden_wide, pullback = jax.vjp(
            lambda values: modulate(values, text_mask, text_count), widened
        )
        hidden_layer_state = hidden_wide.astype(jnp.bfloat16)
        gate_preactivation = jnp.dot(
            hidden_layer_state, weight_fwd, preferred_element_type=jnp.float32
        )
        derivative_rows = (grad_rows.astype(jnp.float32) * silu_slope(gate_preactivation)).astype(
            jnp.bfloat16
        )
        reverse_sweep = lax.dot_general(
            derivative_rows,
            weight_fwd,
            (((1,), (1,)), ((), ())),
            preferred_element_type=jnp.float32,
        )
        grad_out = (grad_rows.astype(jnp.float32) + pullback(reverse_sweep)[0]).astype(jnp.bfloat16)
        return (grad_out, hidden_layer_state, derivative_rows)

    def retreat(turn_index, grad_in, top_slot, saved_rows):
        micro_idx = turn_index - (PIPE - 1 - section_pos)
        active = (micro_idx >= 0) & (micro_idx < PIPE)
        clipped = jnp.clip(micro_idx, 0, PIPE - 1)
        grad_rows = jnp.where(section_pos == PIPE - 1, top_slot, grad_in)

        def retreat_do_work(kept):
            tokens_in = lax.dynamic_index_in_dim(stored, clipped, 0, keepdims=False)
            grad_out, hidden_layer_state, derivative_rows = backward(
                tokens_in, grad_rows, micro_idx
            )
            hiddens = lax.dynamic_update_index_in_dim(kept[0], hidden_layer_state, clipped, 0)
            slopes = lax.dynamic_update_index_in_dim(kept[1], derivative_rows, clipped, 0)
            return (grad_out, (hiddens, slopes))

        def retreat_no_work(kept):
            return (zero_rows, kept)

        return lax.cond(active, retreat_do_work, retreat_no_work, saved_rows)

    top_slot = top_grad[0, 0]
    saved_rows = (jnp.zeros_like(stored), jnp.zeros_like(stored))
    outbox, saved_rows = retreat(0, zero_rows, top_slot, saved_rows)

    def both_backward(turn_index, state_tuple):
        top_slot, outbox, saved_rows = state_tuple
        grad_in, top_slot = neighbours(outbox, top_slot)
        outbox, saved_rows = retreat(turn_index, grad_in, top_slot, saved_rows)
        return (top_slot, outbox, saved_rows)

    state_tuple = lax.fori_loop(1, final_turn, both_backward, (top_slot, outbox, saved_rows))
    hiddens, slopes = state_tuple[2]
    flat_hidden = hiddens.reshape(-1, hiddens.shape[-1])
    flat_slope = slopes.reshape(-1, slopes.shape[-1])
    my_share = lax.psum_scatter(
        lax.dot_general(
            flat_hidden, flat_slope, (((0,), (0,)), ((), ())), preferred_element_type=jnp.float32
        ).astype(jnp.bfloat16),
        "dp",
        scatter_dimension=0,
        tiled=True,
    ).astype(jnp.float32)
    return my_share[None]


def solution(mesh):
    placed = (
        P("section", None, "dp", None),
        P("section", None, "dp", None),
        P(),
        P(),
        P(),
        P(),
        P("section", "dp", None),
        P("dp", "section", None, None),
    )
    return jax.shard_map(
        local, mesh=mesh, in_specs=placed, out_specs=P("section", "dp", None), check_vma=False
    )
```

profile of v0, /device:TPU:1, one launch (start us, length us, event | category | flops | bytes accessed | tf_op | source)
XLA Modules:
  0.0 691.9 jit_solution(8392357912721677020)
XLA Ops:
  10.6 4.6 convolution_convert_fusion
  17.6 13.8 %all-to-all-start.1 = ((bf16[16,2,512]{2,1,0:T(2,128)(2,1)}), bf16[16,2,512]{2,1,0:T(2,128)(2,1)S(1)}, u32[]{:S(2)}, u32[]{:S(2)}) async-start(bf16[16,2,512]{2,1,0:T(2,128)(2,1)} %reshape.240), calls=%async_computation.1 | async-start | bytes 65536 | tf_op jit(solution)/shard_map/all_to_all | solution.py:63
  33.5 5.4 all-to-all-done.1
  42.8 7.3 %all-to-all-done = bf16[16,2,512]{2,1,0:T(2,128)(2,1)S(1)} async-done(((bf16[16,2,512]{2,1,0:T(2,128)(2,1)}), bf16[16,2,512]{2,1,0:T(2,128)(2,1)S(1)}, u32[]{:S(2)}, u32[]{:S(2)}) %all-to-all-start) | async-done | bytes 32800 | tf_op jit(solution)/shard_map/all_to_all | solution.py:62
  50.1 12.0 %all-gather.3.cloned.1.call-done = bf16[1,1024,1024]{2,1,0:T(8,128)(2,1)} async-done(((bf16[1,64,1024]{2,1,0:T(8,128)(2,1)}), bf16[1,1024,1024]{2,1,0:T(8,128)(2,1)}) %all-gather.3.cloned.1.call-update) | async-done | bytes 2097168 | tf_op jit(solution)/shard_map/all_gather | solution.py:70
  62.1 6.4 conditional.4
  68.6 166.7 %while.46 = (s32[]{:T(128)}, bf16[32,1024]{1,0:T(8,128)(2,1)S(1)}, bf16[32,1024]{1,0:T(8,128)(2,1)}, bf16[8,32,1024]{2,1,0:T(8,128)(2,1)}, s32[]{:T(128)}, /*ind...) while((s32[]{:T(128)}, bf16[32,1024]{1,0:T(8,128)(2,1)S(1)}, ...), condition=%wide.region_10.12_spmd.clone.clone, body=%wide.region_5.11_spmd.clone.clone.sunk | while | flops 67733672 | bytes 3295359 | solution.py:120
  75.5 5.5 conditional.12
  88.2 5.5 conditional.12
  95.0 4.5 collective-permute-start.1
  101.1 5.5 conditional.12
  113.8 5.5 conditional.12
  126.5 5.5 conditional.12
  139.2 5.5 conditional.12
  146.0 4.5 collective-permute-start.1
  152.1 5.5 conditional.12
  158.9 5.4 collective-permute-start.1
  167.9 10.3 %collective-permute-start.1 = (bf16[1,32,1024]{2,1,0:T(8,128)(2,1)}, bf16[1,32,1024]{2,1,0:T(8,128)(2,1)S(1)}, u32[]{:S(2)}, u32[]{:S(2)}) collective-permute-start(bf16[1,32,1024]{2,1,0:T(8,128)(2,1)} %bitcast.153), channel_id=1, source_target_pairs={{0,1},{1,2},{2,3},{3,4},{4,5},{5,6},{6,7},{7,8},{8,9},{9,10},{10,1... | collective-permute-start | bytes 196616 | tf_op jit(solution)/shard_map/while/body/eval_jaxpr/ppermute | solution.py:21
  181.8 5.4 collective-permute-start.1
  190.8 10.3 %collective-permute-start.1 = (bf16[1,32,1024]{2,1,0:T(8,128)(2,1)}, bf16[1,32,1024]{2,1,0:T(8,128)(2,1)S(1)}, u32[]{:S(2)}, u32[]{:S(2)}) collective-permute-start(bf16[1,32,1024]{2,1,0:T(8,128)(2,1)} %bitcast.153), channel_id=1, source_target_pairs={{0,1},{1,2},{2,3},{3,4},{4,5},{5,6},{6,7},{7,8},{8,9},{9,10},{10,1... | collective-permute-start | bytes 196616 | tf_op jit(solution)/shard_map/while/body/eval_jaxpr/ppermute | solution.py:21
  204.7 5.4 collective-permute-start.1
  213.7 10.3 %collective-permute-start.1 = (bf16[1,32,1024]{2,1,0:T(8,128)(2,1)}, bf16[1,32,1024]{2,1,0:T(8,128)(2,1)S(1)}, u32[]{:S(2)}, u32[]{:S(2)}) collective-permute-start(bf16[1,32,1024]{2,1,0:T(8,128)(2,1)} %bitcast.153), channel_id=1, source_target_pairs={{0,1},{1,2},{2,3},{3,4},{4,5},{5,6},{6,7},{7,8},{8,9},{9,10},{10,1... | collective-permute-start | bytes 196616 | tf_op jit(solution)/shard_map/while/body/eval_jaxpr/ppermute | solution.py:21
  227.9 5.1 collective-permute-start.1
  237.6 342.0 %while.47 = (s32[]{:T(128)}, bf16[32,1024]{1,0:T(8,128)(2,1)S(1)}, bf16[32,1024]{1,0:T(8,128)(2,1)}, bf16[8,32,1024]{2,1,0:T(8,128)(2,1)}, bf16[8,32,1024]{2,1,0...) while((s32[]{:T(128)}, bf16[32,1024]{1,0:T(8,128)(2,1)S(1)}, ...), condition=%wide.region_24.26_spmd.clone.clone, body=%wide.region_17.25_spmd.clone.clone.sunk | while | flops 136088896 | bytes 14930411 | solution.py:175
  237.6 10.0 %collective-permute-start.2 = (bf16[1,32,1024]{2,1,0:T(8,128)(2,1)S(1)}, bf16[1,32,1024]{2,1,0:T(8,128)(2,1)S(1)}, u32[]{:S(2)}, u32[]{:S(2)}) collective-permute-start(bf16[1,32,1024]{2,1,0:T(8,128)(2,1)S(1)} %bitcast.165), channel_id=1, source_target_pairs={{0,1},{1,2},{2,3},{3,4},{4,5},{5,6},{6,7},{7,8},{8,9},{9,10},{10,1... | collective-permute-start | bytes 196616 | tf_op jit(solution)/shard_map/while/body/eval_jaxpr/ppermute | solution.py:21
  249.0 5.2 collective-permute-done.3
  254.8 7.4 %collective-permute-start.2 = (bf16[1,32,1024]{2,1,0:T(8,128)(2,1)S(1)}, bf16[1,32,1024]{2,1,0:T(8,128)(2,1)S(1)}, u32[]{:S(2)}, u32[]{:S(2)}) collective-permute-start(bf16[1,32,1024]{2,1,0:T(8,128)(2,1)S(1)} %bitcast.165), channel_id=1, source_target_pairs={{0,1},{1,2},{2,3},{3,4},{4,5},{5,6},{6,7},{7,8},{8,9},{9,10},{10,1... | collective-permute-start | bytes 196616 | tf_op jit(solution)/shard_map/while/body/eval_jaxpr/ppermute | solution.py:21
  263.5 5.3 collective-permute-done.3
  269.5 7.5 %collective-permute-start.2 = (bf16[1,32,1024]{2,1,0:T(8,128)(2,1)S(1)}, bf16[1,32,1024]{2,1,0:T(8,128)(2,1)S(1)}, u32[]{:S(2)}, u32[]{:S(2)}) collective-permute-start(bf16[1,32,1024]{2,1,0:T(8,128)(2,1)S(1)} %bitcast.165), channel_id=1, source_target_pairs={{0,1},{1,2},{2,3},{3,4},{4,5},{5,6},{6,7},{7,8},{8,9},{9,10},{10,1... | collective-permute-start | bytes 196616 | tf_op jit(solution)/shard_map/while/body/eval_jaxpr/ppermute | solution.py:21
  278.3 4.9 collective-permute-done.3
  283.9 21.4 %collective-permute-start.2 = (bf16[1,32,1024]{2,1,0:T(8,128)(2,1)S(1)}, bf16[1,32,1024]{2,1,0:T(8,128)(2,1)S(1)}, u32[]{:S(2)}, u32[]{:S(2)}) collective-permute-start(bf16[1,32,1024]{2,1,0:T(8,128)(2,1)S(1)} %bitcast.165), channel_id=1, source_target_pairs={{0,1},{1,2},{2,3},{3,4},{4,5},{5,6},{6,7},{7,8},{8,9},{9,10},{10,1... | collective-permute-start | bytes 196616 | tf_op jit(solution)/shard_map/while/body/eval_jaxpr/ppermute | solution.py:21
  306.6 15.8 %collective-permute-done.3 = bf16[1,32,1024]{2,1,0:T(8,128)(2,1)S(1)} collective-permute-done((bf16[1,32,1024]{2,1,0:T(8,128)(2,1)}, bf16[1,32,1024]{2,1,0:T(8,128)(2,1)S(1)}, u32[]{:S(2)}, u32[]{:S(2)}) %collective-permute-start.3) | collective-permute-done | bytes 65568 | tf_op jit(solution)/shard_map/while/body/eval_jaxpr/ppermute | solution.py:23
  323.1 15.3 %collective-permute-start.2 = (bf16[1,32,1024]{2,1,0:T(8,128)(2,1)S(1)}, bf16[1,32,1024]{2,1,0:T(8,128)(2,1)S(1)}, u32[]{:S(2)}, u32[]{:S(2)}) collective-permute-start(bf16[1,32,1024]{2,1,0:T(8,128)(2,1)S(1)} %bitcast.165), channel_id=1, source_target_pairs={{0,1},{1,2},{2,3},{3,4},{4,5},{5,6},{6,7},{7,8},{8,9},{9,10},{10,1... | collective-permute-start | bytes 196616 | tf_op jit(solution)/shard_map/while/body/eval_jaxpr/ppermute | solution.py:21
  339.7 15.8 %collective-permute-done.3 = bf16[1,32,1024]{2,1,0:T(8,128)(2,1)S(1)} collective-permute-done((bf16[1,32,1024]{2,1,0:T(8,128)(2,1)}, bf16[1,32,1024]{2,1,0:T(8,128)(2,1)S(1)}, u32[]{:S(2)}, u32[]{:S(2)}) %collective-permute-start.3) | collective-permute-done | bytes 65568 | tf_op jit(solution)/shard_map/while/body/eval_jaxpr/ppermute | solution.py:23
  356.2 16.5 %collective-permute-start.2 = (bf16[1,32,1024]{2,1,0:T(8,128)(2,1)S(1)}, bf16[1,32,1024]{2,1,0:T(8,128)(2,1)S(1)}, u32[]{:S(2)}, u32[]{:S(2)}) collective-permute-start(bf16[1,32,1024]{2,1,0:T(8,128)(2,1)S(1)} %bitcast.165), channel_id=1, source_target_pairs={{0,1},{1,2},{2,3},{3,4},{4,5},{5,6},{6,7},{7,8},{8,9},{9,10},{10,1... | collective-permute-start | bytes 196616 | tf_op jit(solution)/shard_map/while/body/eval_jaxpr/ppermute | solution.py:21
  374.0 15.8 %collective-permute-done.3 = bf16[1,32,1024]{2,1,0:T(8,128)(2,1)S(1)} collective-permute-done((bf16[1,32,1024]{2,1,0:T(8,128)(2,1)}, bf16[1,32,1024]{2,1,0:T(8,128)(2,1)S(1)}, u32[]{:S(2)}, u32[]{:S(2)}) %collective-permute-start.3) | collective-permute-done | bytes 65568 | tf_op jit(solution)/shard_map/while/body/eval_jaxpr/ppermute | solution.py:23
  390.5 15.8 %collective-permute-start.2 = (bf16[1,32,1024]{2,1,0:T(8,128)(2,1)S(1)}, bf16[1,32,1024]{2,1,0:T(8,128)(2,1)S(1)}, u32[]{:S(2)}, u32[]{:S(2)}) collective-permute-start(bf16[1,32,1024]{2,1,0:T(8,128)(2,1)S(1)} %bitcast.165), channel_id=1, source_target_pairs={{0,1},{1,2},{2,3},{3,4},{4,5},{5,6},{6,7},{7,8},{8,9},{9,10},{10,1... | collective-permute-start | bytes 196616 | tf_op jit(solution)/shard_map/while/body/eval_jaxpr/ppermute | solution.py:21
  411.5 12.6 %conditional.13 = (bf16[32,1024]{1,0:T(8,128)(2,1)}, bf16[8,32,1024]{2,1,0:T(8,128)(2,1)}, bf16[8,32,1024]{2,1,0:T(8,128)(2,1)}) conditional(s32[]{:T(128)} %convert_element_type.366, (bf16[8,32,1024]{2,1,0:T(8,128)(2,1)}, bf16[8,32,1024]{2,1,0:T(8,128)(2,1)}) %tuple.144, (pred[]{:T(512)}, bf16[1,32,1024]{2,1,0:T(8,128)(2,1)S(1)}, ...), branch_computations={%region_18.19_spmd, %region_19.24_spmd} | conditional | flops 136088896 | bytes 14274576 | solution.py:163
  432.7 12.6 %conditional.13 = (bf16[32,1024]{1,0:T(8,128)(2,1)}, bf16[8,32,1024]{2,1,0:T(8,128)(2,1)}, bf16[8,32,1024]{2,1,0:T(8,128)(2,1)}) conditional(s32[]{:T(128)} %convert_element_type.366, (bf16[8,32,1024]{2,1,0:T(8,128)(2,1)}, bf16[8,32,1024]{2,1,0:T(8,128)(2,1)}) %tuple.144, (pred[]{:T(512)}, bf16[1,32,1024]{2,1,0:T(8,128)(2,1)S(1)}, ...), branch_computations={%region_18.19_spmd, %region_19.24_spmd} | conditional | flops 136088896 | bytes 14274576 | solution.py:163
  454.0 12.6 %conditional.13 = (bf16[32,1024]{1,0:T(8,128)(2,1)}, bf16[8,32,1024]{2,1,0:T(8,128)(2,1)}, bf16[8,32,1024]{2,1,0:T(8,128)(2,1)}) conditional(s32[]{:T(128)} %convert_element_type.366, (bf16[8,32,1024]{2,1,0:T(8,128)(2,1)}, bf16[8,32,1024]{2,1,0:T(8,128)(2,1)}) %tuple.144, (pred[]{:T(512)}, bf16[1,32,1024]{2,1,0:T(8,128)(2,1)S(1)}, ...), branch_computations={%region_18.19_spmd, %region_19.24_spmd} | conditional | flops 136088896 | bytes 14274576 | solution.py:163
  475.0 12.6 %conditional.13 = (bf16[32,1024]{1,0:T(8,128)(2,1)}, bf16[8,32,1024]{2,1,0:T(8,128)(2,1)}, bf16[8,32,1024]{2,1,0:T(8,128)(2,1)}) conditional(s32[]{:T(128)} %convert_element_type.366, (bf16[8,32,1024]{2,1,0:T(8,128)(2,1)}, bf16[8,32,1024]{2,1,0:T(8,128)(2,1)}) %tuple.144, (pred[]{:T(512)}, bf16[1,32,1024]{2,1,0:T(8,128)(2,1)S(1)}, ...), branch_computations={%region_18.19_spmd, %region_19.24_spmd} | conditional | flops 136088896 | bytes 14274576 | solution.py:163
  487.6 9.8 %collective-permute-start.2 = (bf16[1,32,1024]{2,1,0:T(8,128)(2,1)S(1)}, bf16[1,32,1024]{2,1,0:T(8,128)(2,1)S(1)}, u32[]{:S(2)}, u32[]{:S(2)}) collective-permute-start(bf16[1,32,1024]{2,1,0:T(8,128)(2,1)S(1)} %bitcast.165), channel_id=1, source_target_pairs={{0,1},{1,2},{2,3},{3,4},{4,5},{5,6},{6,7},{7,8},{8,9},{9,10},{10,1... | collective-permute-start | bytes 196616 | tf_op jit(solution)/shard_map/while/body/eval_jaxpr/ppermute | solution.py:21
  502.6 12.6 %conditional.13 = (bf16[32,1024]{1,0:T(8,128)(2,1)}, bf16[8,32,1024]{2,1,0:T(8,128)(2,1)}, bf16[8,32,1024]{2,1,0:T(8,128)(2,1)}) conditional(s32[]{:T(128)} %convert_element_type.366, (bf16[8,32,1024]{2,1,0:T(8,128)(2,1)}, bf16[8,32,1024]{2,1,0:T(8,128)(2,1)}) %tuple.144, (pred[]{:T(512)}, bf16[1,32,1024]{2,1,0:T(8,128)(2,1)S(1)}, ...), branch_computations={%region_18.19_spmd, %region_19.24_spmd} | conditional | flops 136088896 | bytes 14274576 | solution.py:163
  515.1 4.4 collective-permute-start.2
  524.8 12.6 %conditional.13 = (bf16[32,1024]{1,0:T(8,128)(2,1)}, bf16[8,32,1024]{2,1,0:T(8,128)(2,1)}, bf16[8,32,1024]{2,1,0:T(8,128)(2,1)}) conditional(s32[]{:T(128)} %convert_element_type.366, (bf16[8,32,1024]{2,1,0:T(8,128)(2,1)}, bf16[8,32,1024]{2,1,0:T(8,128)(2,1)}) %tuple.144, (pred[]{:T(512)}, bf16[1,32,1024]{2,1,0:T(8,128)(2,1)S(1)}, ...), branch_computations={%region_18.19_spmd, %region_19.24_spmd} | conditional | flops 136088896 | bytes 14274576 | solution.py:163
  545.9 12.6 %conditional.13 = (bf16[32,1024]{1,0:T(8,128)(2,1)}, bf16[8,32,1024]{2,1,0:T(8,128)(2,1)}, bf16[8,32,1024]{2,1,0:T(8,128)(2,1)}) conditional(s32[]{:T(128)} %convert_element_type.366, (bf16[8,32,1024]{2,1,0:T(8,128)(2,1)}, bf16[8,32,1024]{2,1,0:T(8,128)(2,1)}) %tuple.144, (pred[]{:T(512)}, bf16[1,32,1024]{2,1,0:T(8,128)(2,1)S(1)}, ...), branch_computations={%region_18.19_spmd, %region_19.24_spmd} | conditional | flops 136088896 | bytes 14274576 | solution.py:163
  567.1 12.6 %conditional.13 = (bf16[32,1024]{1,0:T(8,128)(2,1)}, bf16[8,32,1024]{2,1,0:T(8,128)(2,1)}, bf16[8,32,1024]{2,1,0:T(8,128)(2,1)}) conditional(s32[]{:T(128)} %convert_element_type.366, (bf16[8,32,1024]{2,1,0:T(8,128)(2,1)}, bf16[8,32,1024]{2,1,0:T(8,128)(2,1)}) %tuple.144, (pred[]{:T(512)}, bf16[1,32,1024]{2,1,0:T(8,128)(2,1)S(1)}, ...), branch_computations={%region_18.19_spmd, %region_19.24_spmd} | conditional | flops 136088896 | bytes 14274576 | solution.py:163
  583.0 100.5 %reduce-scatter.2.cloned.1.call-done = bf16[64,1024]{1,0:T(8,128)(2,1)} async-done(((bf16[1024,1024]{1,0:T(8,128)(2,1)}), bf16[64,1024]{1,0:T(8,128)(2,1)}) %reduce-scatter.2.cloned.1.call-update) | async-done | bytes 131088 | tf_op jit(solution)/shard_map/reduce_scatter | solution.py:179
  (401 shorter events, 290.6 us)
Async XLA Ops:
  6.5 55.6 %all-gather.3.cloned.1.call-start = ((), (), s32[]{:S(2)}) async-start(), calls=%async_computation.4 | async-start | bytes 2228224 | tf_op jit(solution)/shard_map/all_gather | solution.py:70
  17.6 21.2 %all-to-all-start.1 = ((bf16[16,2,512]{2,1,0:T(2,128)(2,1)}), bf16[16,2,512]{2,1,0:T(2,128)(2,1)S(1)}, u32[]{:S(2)}, u32[]{:S(2)}) async-start(bf16[16,2,512]{2,1,0:T(2,128)(2,1)} %reshape.240), calls=%async_computation.1 | async-start | bytes 65536 | tf_op jit(solution)/shard_map/all_to_all | solution.py:63
  38.9 11.2 %all-to-all-start = ((bf16[16,2,512]{2,1,0:T(2,128)(2,1)}), bf16[16,2,512]{2,1,0:T(2,128)(2,1)S(1)}, u32[]{:S(2)}, u32[]{:S(2)}) async-start(bf16[16,2,512]{2,1,0:T(2,128)(2,1)} %reshape.242), calls=%async_computation | async-start | bytes 65536 | tf_op jit(solution)/shard_map/all_to_all | solution.py:62
  42.6 640.9 %reduce-scatter.2.cloned.1.call-start = ((), (), s32[]{:S(2)}) async-start(), calls=%async_computation.3 | async-start | bytes 2228224 | tf_op jit(solution)/shard_map/reduce_scatter | solution.py:179
  68.6 5.3 collective-permute-start
  69.8 5.6 collective-permute-start.1
  81.0 5.5 collective-permute-start
  82.3 5.8 collective-permute-start.1
  93.7 5.8 collective-permute-start
  95.0 6.1 collective-permute-start.1
  106.7 5.5 collective-permute-start
  108.0 5.9 collective-permute-start.1
  119.4 5.5 collective-permute-start
  120.6 5.8 collective-permute-start.1
  132.0 5.5 collective-permute-start
  133.3 5.9 collective-permute-start.1
  144.7 5.8 collective-permute-start
  146.0 6.1 collective-permute-start.1
  157.6 6.7 collective-permute-start
  158.9 7.1 %collective-permute-start.1 = (bf16[1,32,1024]{2,1,0:T(8,128)(2,1)}, bf16[1,32,1024]{2,1,0:T(8,128)(2,1)S(1)}, u32[]{:S(2)}, u32[]{:S(2)}) collective-permute-start(bf16[1,32,1024]{2,1,0:T(8,128)(2,1)} %bitcast.153), channel_id=1, source_target_pairs={{0,1},{1,2},{2,3},{3,4},{4,5},{5,6},{6,7},{7,8},{8,9},{9,10},{10,1... | collective-permute-start | bytes 196616 | tf_op jit(solution)/shard_map/while/body/eval_jaxpr/ppermute | solution.py:21
  166.6 11.6 %collective-permute-start = (bf16[1,32,1024]{2,1,0:T(8,128)(2,1)S(1)}, bf16[1,32,1024]{2,1,0:T(8,128)(2,1)S(1)}, u32[]{:S(2)}, u32[]{:S(2)}) collective-permute-start(bf16[1,32,1024]{2,1,0:T(8,128)(2,1)S(1)} %bitcast.166), channel_id=1, source_target_pairs={{1,0},{2,1},{3,2},{4,3},{5,4},{6,5},{7,6},{8,7},{9,8},{10,9},{11,1... | collective-permute-start | bytes 196616 | tf_op jit(solution)/shard_map/while/body/eval_jaxpr/ppermute | solution.py:23
  167.9 12.0 %collective-permute-start.1 = (bf16[1,32,1024]{2,1,0:T(8,128)(2,1)}, bf16[1,32,1024]{2,1,0:T(8,128)(2,1)S(1)}, u32[]{:S(2)}, u32[]{:S(2)}) collective-permute-start(bf16[1,32,1024]{2,1,0:T(8,128)(2,1)} %bitcast.153), channel_id=1, source_target_pairs={{0,1},{1,2},{2,3},{3,4},{4,5},{5,6},{6,7},{7,8},{8,9},{9,10},{10,1... | collective-permute-start | bytes 196616 | tf_op jit(solution)/shard_map/while/body/eval_jaxpr/ppermute | solution.py:21
  180.5 6.7 collective-permute-start
  181.8 7.1 %collective-permute-start.1 = (bf16[1,32,1024]{2,1,0:T(8,128)(2,1)}, bf16[1,32,1024]{2,1,0:T(8,128)(2,1)S(1)}, u32[]{:S(2)}, u32[]{:S(2)}) collective-permute-start(bf16[1,32,1024]{2,1,0:T(8,128)(2,1)} %bitcast.153), channel_id=1, source_target_pairs={{0,1},{1,2},{2,3},{3,4},{4,5},{5,6},{6,7},{7,8},{8,9},{9,10},{10,1... | collective-permute-start | bytes 196616 | tf_op jit(solution)/shard_map/while/body/eval_jaxpr/ppermute | solution.py:21
  189.5 11.6 %collective-permute-start = (bf16[1,32,1024]{2,1,0:T(8,128)(2,1)S(1)}, bf16[1,32,1024]{2,1,0:T(8,128)(2,1)S(1)}, u32[]{:S(2)}, u32[]{:S(2)}) collective-permute-start(bf16[1,32,1024]{2,1,0:T(8,128)(2,1)S(1)} %bitcast.166), channel_id=1, source_target_pairs={{1,0},{2,1},{3,2},{4,3},{5,4},{6,5},{7,6},{8,7},{9,8},{10,9},{11,1... | collective-permute-start | bytes 196616 | tf_op jit(solution)/shard_map/while/body/eval_jaxpr/ppermute | solution.py:23
  190.8 12.0 %collective-permute-start.1 = (bf16[1,32,1024]{2,1,0:T(8,128)(2,1)}, bf16[1,32,1024]{2,1,0:T(8,128)(2,1)S(1)}, u32[]{:S(2)}, u32[]{:S(2)}) collective-permute-start(bf16[1,32,1024]{2,1,0:T(8,128)(2,1)} %bitcast.153), channel_id=1, source_target_pairs={{0,1},{1,2},{2,3},{3,4},{4,5},{5,6},{6,7},{7,8},{8,9},{9,10},{10,1... | collective-permute-start | bytes 196616 | tf_op jit(solution)/shard_map/while/body/eval_jaxpr/ppermute | solution.py:21
  203.4 6.7 collective-permute-start
  204.7 7.1 %collective-permute-start.1 = (bf16[1,32,1024]{2,1,0:T(8,128)(2,1)}, bf16[1,32,1024]{2,1,0:T(8,128)(2,1)S(1)}, u32[]{:S(2)}, u32[]{:S(2)}) collective-permute-start(bf16[1,32,1024]{2,1,0:T(8,128)(2,1)} %bitcast.153), channel_id=1, source_target_pairs={{0,1},{1,2},{2,3},{3,4},{4,5},{5,6},{6,7},{7,8},{8,9},{9,10},{10,1... | collective-permute-start | bytes 196616 | tf_op jit(solution)/shard_map/while/body/eval_jaxpr/ppermute | solution.py:21
  212.4 11.6 %collective-permute-start = (bf16[1,32,1024]{2,1,0:T(8,128)(2,1)S(1)}, bf16[1,32,1024]{2,1,0:T(8,128)(2,1)S(1)}, u32[]{:S(2)}, u32[]{:S(2)}) collective-permute-start(bf16[1,32,1024]{2,1,0:T(8,128)(2,1)S(1)} %bitcast.166), channel_id=1, source_target_pairs={{1,0},{2,1},{3,2},{4,3},{5,4},{6,5},{7,6},{8,7},{9,8},{10,9},{11,1... | collective-permute-start | bytes 196616 | tf_op jit(solution)/shard_map/while/body/eval_jaxpr/ppermute | solution.py:23
  213.7 12.3 %collective-permute-start.1 = (bf16[1,32,1024]{2,1,0:T(8,128)(2,1)}, bf16[1,32,1024]{2,1,0:T(8,128)(2,1)S(1)}, u32[]{:S(2)}, u32[]{:S(2)}) collective-permute-start(bf16[1,32,1024]{2,1,0:T(8,128)(2,1)} %bitcast.153), channel_id=1, source_target_pairs={{0,1},{1,2},{2,3},{3,4},{4,5},{5,6},{6,7},{7,8},{8,9},{9,10},{10,1... | collective-permute-start | bytes 196616 | tf_op jit(solution)/shard_map/while/body/eval_jaxpr/ppermute | solution.py:21
  226.6 6.4 collective-permute-start
  227.9 6.7 collective-permute-start.1
  237.6 11.3 %collective-permute-start.2 = (bf16[1,32,1024]{2,1,0:T(8,128)(2,1)S(1)}, bf16[1,32,1024]{2,1,0:T(8,128)(2,1)S(1)}, u32[]{:S(2)}, u32[]{:S(2)}) collective-permute-start(bf16[1,32,1024]{2,1,0:T(8,128)(2,1)S(1)} %bitcast.165), channel_id=1, source_target_pairs={{0,1},{1,2},{2,3},{3,4},{4,5},{5,6},{6,7},{7,8},{8,9},{9,10},{10,1... | collective-permute-start | bytes 196616 | tf_op jit(solution)/shard_map/while/body/eval_jaxpr/ppermute | solution.py:21
  247.7 6.5 collective-permute-start.3
  254.8 8.7 %collective-permute-start.2 = (bf16[1,32,1024]{2,1,0:T(8,128)(2,1)S(1)}, bf16[1,32,1024]{2,1,0:T(8,128)(2,1)S(1)}, u32[]{:S(2)}, u32[]{:S(2)}) collective-permute-start(bf16[1,32,1024]{2,1,0:T(8,128)(2,1)S(1)} %bitcast.165), channel_id=1, source_target_pairs={{0,1},{1,2},{2,3},{3,4},{4,5},{5,6},{6,7},{7,8},{8,9},{9,10},{10,1... | collective-permute-start | bytes 196616 | tf_op jit(solution)/shard_map/while/body/eval_jaxpr/ppermute | solution.py:21
  262.2 6.7 collective-permute-start.3
  269.5 8.8 %collective-permute-start.2 = (bf16[1,32,1024]{2,1,0:T(8,128)(2,1)S(1)}, bf16[1,32,1024]{2,1,0:T(8,128)(2,1)S(1)}, u32[]{:S(2)}, u32[]{:S(2)}) collective-permute-start(bf16[1,32,1024]{2,1,0:T(8,128)(2,1)S(1)} %bitcast.165), channel_id=1, source_target_pairs={{0,1},{1,2},{2,3},{3,4},{4,5},{5,6},{6,7},{7,8},{8,9},{9,10},{10,1... | collective-permute-start | bytes 196616 | tf_op jit(solution)/shard_map/while/body/eval_jaxpr/ppermute | solution.py:21
  277.0 6.2 collective-permute-start.3
  283.9 22.7 %collective-permute-start.2 = (bf16[1,32,1024]{2,1,0:T(8,128)(2,1)S(1)}, bf16[1,32,1024]{2,1,0:T(8,128)(2,1)S(1)}, u32[]{:S(2)}, u32[]{:S(2)}) collective-permute-start(bf16[1,32,1024]{2,1,0:T(8,128)(2,1)S(1)} %bitcast.165), channel_id=1, source_target_pairs={{0,1},{1,2},{2,3},{3,4},{4,5},{5,6},{6,7},{7,8},{8,9},{9,10},{10,1... | collective-permute-start | bytes 196616 | tf_op jit(solution)/shard_map/while/body/eval_jaxpr/ppermute | solution.py:21
  305.3 17.2 %collective-permute-start.3 = (bf16[1,32,1024]{2,1,0:T(8,128)(2,1)}, bf16[1,32,1024]{2,1,0:T(8,128)(2,1)S(1)}, u32[]{:S(2)}, u32[]{:S(2)}) collective-permute-start(bf16[1,32,1024]{2,1,0:T(8,128)(2,1)} %bitcast.156), channel_id=1, source_target_pairs={{1,0},{2,1},{3,2},{4,3},{5,4},{6,5},{7,6},{8,7},{9,8},{10,9},{11,1... | collective-permute-start | bytes 196616 | tf_op jit(solution)/shard_map/while/body/eval_jaxpr/ppermute | solution.py:23
  323.1 16.6 %collective-permute-start.2 = (bf16[1,32,1024]{2,1,0:T(8,128)(2,1)S(1)}, bf16[1,32,1024]{2,1,0:T(8,128)(2,1)S(1)}, u32[]{:S(2)}, u32[]{:S(2)}) collective-permute-start(bf16[1,32,1024]{2,1,0:T(8,128)(2,1)S(1)} %bitcast.165), channel_id=1, source_target_pairs={{0,1},{1,2},{2,3},{3,4},{4,5},{5,6},{6,7},{7,8},{8,9},{9,10},{10,1... | collective-permute-start | bytes 196616 | tf_op jit(solution)/shard_map/while/body/eval_jaxpr/ppermute | solution.py:21
  338.4 17.2 %collective-permute-start.3 = (bf16[1,32,1024]{2,1,0:T(8,128)(2,1)}, bf16[1,32,1024]{2,1,0:T(8,128)(2,1)S(1)}, u32[]{:S(2)}, u32[]{:S(2)}) collective-permute-start(bf16[1,32,1024]{2,1,0:T(8,128)(2,1)} %bitcast.156), channel_id=1, source_target_pairs={{1,0},{2,1},{3,2},{4,3},{5,4},{6,5},{7,6},{8,7},{9,8},{10,9},{11,1... | collective-permute-start | bytes 196616 | tf_op jit(solution)/shard_map/while/body/eval_jaxpr/ppermute | solution.py:23
  356.2 17.8 %collective-permute-start.2 = (bf16[1,32,1024]{2,1,0:T(8,128)(2,1)S(1)}, bf16[1,32,1024]{2,1,0:T(8,128)(2,1)S(1)}, u32[]{:S(2)}, u32[]{:S(2)}) collective-permute-start(bf16[1,32,1024]{2,1,0:T(8,128)(2,1)S(1)} %bitcast.165), channel_id=1, source_target_pairs={{0,1},{1,2},{2,3},{3,4},{4,5},{5,6},{6,7},{7,8},{8,9},{9,10},{10,1... | collective-permute-start | bytes 196616 | tf_op jit(solution)/shard_map/while/body/eval_jaxpr/ppermute | solution.py:21
  372.7 17.2 %collective-permute-start.3 = (bf16[1,32,1024]{2,1,0:T(8,128)(2,1)}, bf16[1,32,1024]{2,1,0:T(8,128)(2,1)S(1)}, u32[]{:S(2)}, u32[]{:S(2)}) collective-permute-start(bf16[1,32,1024]{2,1,0:T(8,128)(2,1)} %bitcast.156), channel_id=1, source_target_pairs={{1,0},{2,1},{3,2},{4,3},{5,4},{6,5},{7,6},{8,7},{9,8},{10,9},{11,1... | collective-permute-start | bytes 196616 | tf_op jit(solution)/shard_map/while/body/eval_jaxpr/ppermute | solution.py:23
  390.5 17.2 %collective-permute-start.2 = (bf16[1,32,1024]{2,1,0:T(8,128)(2,1)S(1)}, bf16[1,32,1024]{2,1,0:T(8,128)(2,1)S(1)}, u32[]{:S(2)}, u32[]{:S(2)}) collective-permute-start(bf16[1,32,1024]{2,1,0:T(8,128)(2,1)S(1)} %bitcast.165), channel_id=1, source_target_pairs={{0,1},{1,2},{2,3},{3,4},{4,5},{5,6},{6,7},{7,8},{8,9},{9,10},{10,1... | collective-permute-start | bytes 196616 | tf_op jit(solution)/shard_map/while/body/eval_jaxpr/ppermute | solution.py:21
  487.6 11.1 %collective-permute-start.2 = (bf16[1,32,1024]{2,1,0:T(8,128)(2,1)S(1)}, bf16[1,32,1024]{2,1,0:T(8,128)(2,1)S(1)}, u32[]{:S(2)}, u32[]{:S(2)}) collective-permute-start(bf16[1,32,1024]{2,1,0:T(8,128)(2,1)S(1)} %bitcast.165), channel_id=1, source_target_pairs={{0,1},{1,2},{2,3},{3,4},{4,5},{5,6},{6,7},{7,8},{8,9},{9,10},{10,1... | collective-permute-start | bytes 196616 | tf_op jit(solution)/shard_map/while/body/eval_jaxpr/ppermute | solution.py:21
  515.1 5.7 collective-permute-start.2
  519.6 5.2 collective-permute-start.3
  (22 other events, 140.4 us)
Sparse Core Ops, SparseCore 0:
  9.7 52.3 all-gather.2
  583.1 100.3 reduce-scatter.1
where the time goes:
time: 697 us; the launch traced here: 692 us
  starting transfers between devices  260 us (37%)
  waiting for transfers between devices  242 us (35%)
  matrix products  65.9 us (9%)
  other arithmetic  61.5 us (9%)
  local copies, waits for them, and re-layouts  26.1 us (4%)
  loops' own time  22.6 us (3%)
  between operations  13.5 us (2%)
    ppermute x28, starting transfers between devices, extended(): lax.ppermute(tail, axis, [(i, (i + 1) % count) for i in range(ends)])  207 us
    reduce_scatter x1, waiting for transfers between devices, local(): lax.psum_scatter(lax.dot_general(flat_hidden, flat_slope, (((0,), (0,)),...  100 us
    ppermute x28, waiting for transfers between devices, extended(): lax.ppermute(head, axis, [((i + 1) % count, i) for i in range(ends)])  94 us
    ppermute x28, starting transfers between devices, extended(): lax.ppermute(head, axis, [((i + 1) % count, i) for i in range(ends)])  36 us
    ppermute x28, waiting for transfers between devices, extended(): lax.ppermute(tail, axis, [(i, (i + 1) % count) for i in range(ends)])  22.6 us
    dot_general x8, matrix products, backward(): jnp.dot(hidden_layer_state, weight_fwd, preferred_element_type=jnp.float32)  22.4 us
    dot_general x8, matrix products, forward(): jnp.dot(hidden_layer_state, weight_fwd, preferred_element_type=jnp.float32)  22.1 us
  transfers between devices with their start and end apart: 60, of which 32 were waited for; matrix products, arithmetic and copies ran while one was open for 2% of the time, Pallas kernels for 0%

commit v1 on v0

v1 whole, which is shorter than its diff:
```python
import functools

import jax
import jax.numpy as jnp
from jax import lax
from jax.experimental import pallas as pl
from jax.experimental.pallas import tpu as pltpu
from jax.sharding import PartitionSpec as P

NORM_EPS = 1e-06
MESH = pl.DeviceIdType.MESH
F32 = jnp.float32
BF16 = jnp.bfloat16
EMB_CHUNKS = 4
FWD_CHUNKS = 2


def step_kernel(
    n_dp,
    pipe,
    owner_ref,
    len_ref,
    lat_ref,
    txt_ref,
    lat_emb_ref,
    emb_hbm,
    w_ref,
    top_ref,
    out_ref,
    emb,
    wfull,
    route_out,
    route_in,
    rows_f32,
    x0,
    coef,
    xin,
    xout,
    gin,
    gout,
    gate_slope,
    hid_send,
    hid,
    slopes,
    partial,
    rs_out,
    rs_in,
    emb_sem,
    route_sem,
    w_send,
    w_recv,
    pw_send,
    pw_recv,
    feed_sem,
    x_send,
    x_recv,
    g_send,
    g_recv,
    h_sem,
    s_sem,
    r_send,
    r_recv,
):
    chips = n_dp // 2
    half_ring = chips // 2
    channels = wfull.shape[0]
    share = channels // n_dp
    half = share // 2
    rows = 2 * n_dp
    me = lax.axis_index("dp")
    section = lax.axis_index("section")
    pos = lax.rem(section, pipe)
    first = section - pos
    last = first + pipe - 1
    chip = lax.div(me, 2)
    core = lax.rem(me, 2)
    partner = chip * 2 + 1 - core
    beside = first + lax.rem(pos + 1, max(pipe, 1))

    def remote(src, dst, send, recv, **where):
        return pltpu.make_async_remote_copy(
            src_ref=src,
            dst_ref=dst,
            send_sem=send,
            recv_sem=recv,
            device_id=where,
            device_id_type=MESH,
        )

    depth = emb.shape[0] // EMB_CHUNKS

    def emb_copy(i):
        part = pl.ds(i * depth, depth)
        return pltpu.make_async_copy(emb_hbm.at[part], emb.at[part], emb_sem.at[i])

    for i in range(EMB_CHUNKS):
        emb_copy(i).start()

    barrier = pltpu.get_barrier_semaphore()
    for k in range(1, n_dp):
        pl.semaphore_signal(
            barrier, inc=1, device_id={"dp": lax.rem(me + k, n_dp)}, device_id_type=MESH
        )
    for k in range(1, pipe):
        pl.semaphore_signal(
            barrier,
            inc=1,
            device_id={"section": first + lax.rem(pos + k, pipe)},
            device_id_type=MESH,
        )

    block = pl.ds(pl.multiple_of(first, pipe), pipe)
    mine = owner_ref[block, :] == me
    counts = jnp.sum(
        jnp.where(mine, len_ref[block, :], 0).astype(F32), axis=1, keepdims=True
    )
    order = lax.broadcasted_iota(jnp.int32, (n_dp, 128), 0).astype(F32)
    for m in range(pipe):
        count = jnp.broadcast_to(counts[m : m + 1, :], (n_dp, 128))
        coef[m] = jnp.where(order < count, 0.5 / count, 0.0)
    spot = lax.broadcasted_iota(jnp.int32, (n_dp, n_dp), 0)
    pick = (spot == owner_ref[pl.ds(section, 1), :]).astype(F32).astype(BF16)

    wfull[pl.ds(pl.multiple_of(me * share, share), share), :] = w_ref[...]
    pl.semaphore_wait(barrier, n_dp - 1 + pipe - 1)

    def w_block(owner_chip, whose, h):
        start = (owner_chip * 2 + whose) * share + h * half
        return wfull.at[pl.ds(pl.multiple_of(start, half), half)]

    def origin(direction, t):
        step = t if direction == 0 else chips - t
        return lax.rem(chip - step + 2 * chips, chips) if direction == 0 else lax.rem(chip + t, chips)

    def ahead(direction):
        step = 1 if direction == 0 else chips - 1
        return lax.rem(chip + step, chips) * 2 + core

    def halves(direction, t):
        if t == half_ring:
            return (direction,)
        return (0, 1)

    def w_hop(direction, t, h):
        src = w_ref.at[pl.ds(h * half, half)] if t == 1 else w_block(origin(direction, t - 1), core, h)
        dst = w_block(origin(direction, t - 1) if t > 1 else chip, core, h)
        return remote(
            src, dst, w_send.at[direction, t - 1, h], w_recv.at[direction, t - 1, h], dp=ahead(direction)
        )

    def w_land(direction, t, h):
        dst = w_block(origin(direction, t), core, h)
        return remote(
            dst, dst, w_send.at[direction, t - 1, h], w_recv.at[direction, t - 1, h], dp=ahead(direction)
        )

    def w_share(direction, t, h):
        blk = w_block(origin(direction, t), core, h)
        return remote(blk, blk, pw_send.at[direction, t, h], pw_recv.at[direction, t, h], dp=partner)

    def w_shared(direction, t, h):
        blk = w_block(origin(direction, t), 1 - core, h)
        return remote(blk, blk, pw_send.at[direction, t, h], pw_recv.at[direction, t, h], dp=partner)

    def w_own():
        blk = wfull.at[pl.ds(pl.multiple_of(me * share, share), share)]
        return remote(w_ref, blk, pw_send.at[0, 0, 0], pw_recv.at[0, 0, 0], dp=partner)

    def w_owned():
        blk = wfull.at[pl.ds(pl.multiple_of(partner * share, share), share)]
        return remote(w_ref, blk, pw_send.at[0, 0, 0], pw_recv.at[0, 0, 0], dp=partner)

    if half_ring:
        for h in (0, 1):
            for direction in (0, 1):
                if h in halves(direction, 1):
                    w_hop(direction, 1, h).start()
    w_own().start()

    def top_feed(slot):
        return remote(top_ref, gin.at[slot], feed_sem.at[0], g_recv.at[slot], section=last)

    @pl.when(pos < pipe - 1)
    def _():
        top_feed(pipe - 1 - pos).start()

    @pl.when(pos == pipe - 1)
    def _():
        gin[0] = top_ref[...]

    def encode(i, so_far):
        emb_copy(i).wait()
        part = pl.ds(i * depth, depth)
        return so_far + jnp.dot(txt_ref[:, part], emb[part, :], preferred_element_type=F32)

    def ring_step(t):
        for h in (0, 1):
            for direction in (0, 1):
                if h in halves(direction, t):
                    w_land(direction, t, h).wait_recv()
                    if t < half_ring and h in halves(direction, t + 1):
                        w_hop(direction, t + 1, h).start()
                    w_share(direction, t, h).start()

    text = jnp.zeros((n_dp, channels), F32)
    for i in range(EMB_CHUNKS):
        text = encode(i, text)
    lat = jnp.dot(lat_ref[...], lat_emb_ref[...], preferred_element_type=F32)
    lat_sel = jnp.dot(pick, lat.astype(BF16), preferred_element_type=F32)
    text_sel = jnp.dot(pick, text.astype(BF16), preferred_element_type=F32)
    for i in range(n_dp):
        route_out[i, 0:1, :] = lat_sel[i : i + 1, :]
        route_out[i, 1:2, :] = text_sel[i : i + 1, :]

    def route(k):
        to = lax.rem(me + k, n_dp)
        return remote(route_out.at[to], route_in.at[me], route_sem.at[0], route_sem.at[1], dp=to)

    for k in range(1, n_dp):
        route(k).start()
    route_in[me] = route_out[me]
    if half_ring:
        ring_step(1)

    several = pl.ds(0, n_dp - 1)
    routed = remote(
        route_out.at[several], route_in.at[several], route_sem.at[0], route_sem.at[1], dp=partner
    )
    routed.wait_recv()
    for i in range(n_dp):
        rows_f32[i : i + 1, :] = route_in[i, 0:1, :]
        rows_f32[n_dp + i : n_dp + i + 1, :] = route_in[i, 1:2, :]
    x0[...] = rows_f32[...].astype(BF16)

    def row_feed(slot):
        return remote(x0, xin.at[slot], feed_sem.at[1], x_recv.at[slot], section=first)

    @pl.when(pos > 0)
    def _():
        row_feed(pos).start()

    @pl.when(pos == 0)
    def _():
        xin[0] = rows_f32[...].astype(BF16)

    for t in range(2, half_ring + 1):
        ring_step(t)
    w_owned().wait_recv()
    for t in range(1, half_ring + 1):
        for h in (0, 1):
            for direction in (0, 1):
                if h in halves(direction, t):
                    w_shared(direction, t, h).wait_recv()

    text_rows = slice(n_dp, rows)
    low = lax.broadcasted_iota(jnp.int32, (rows, 128), 1) < 64
    spread = channels // 128

    def wide(column):
        return jnp.concatenate([column] * spread, axis=1)

    def normed(m):
        x = xin[m].astype(F32)
        inv = lax.rsqrt(jnp.mean(x * x, axis=1, keepdims=True) + NORM_EPS)
        u = x * inv
        pooled = jnp.sum(u[text_rows, :] * wide(coef[m]), axis=0, keepdims=True)
        return x, inv, u, 1.0 + pooled

    cols = channels // FWD_CHUNKS

    def x_hop(m, n):
        part = pl.ds(n * cols, cols)
        return remote(
            xout.at[m, :, part], xin.at[m, :, part], x_send, x_recv.at[m], section=section + 1
        )

    def hid_hop(m):
        return remote(hid_send.at[m], hid.at[1, m], h_sem.at[0], h_sem.at[1], dp=partner)

    def slope_hop(m):
        return remote(slopes.at[0, m], slopes.at[1, m], s_sem.at[0], s_sem.at[1], dp=partner)

    def forward(m, carry):
        @pl.when((pos > 0) | (m > 0))
        def _():
            remote(xout.at[m], xin.at[m], x_send, x_recv.at[m], section=beside).wait_recv()

        x, inv, u, scale = normed(m)
        hidden_wide = u * scale
        hidden = hidden_wide.astype(BF16)
        for n in range(FWD_CHUNKS):
            part = slice(n * cols, (n + 1) * cols)
            pre = jnp.dot(hidden, wfull[:, part], preferred_element_type=F32)
            sig = jax.nn.sigmoid(pre)
            xout[m, :, part] = (x[:, part] + pre * sig).astype(BF16)

            @pl.when(pos < pipe - 1)
            def _():
                x_hop(m, n).start()

            gate_slope[m, :, part] = sig * (1.0 + pre * (1.0 - sig))
        for k in range(chips // 2):
            a = hidden_wide[:, 256 * k : 256 * k + 128]
            b = hidden_wide[:, 256 * k + 128 : 256 * k + 256]
            lo = jnp.where(low, a, pltpu.roll(b, 64, 1))
            hi = jnp.where(low, pltpu.roll(a, 64, 1), b)
            place = slice(128 * k, 128 * k + 128)
            is_low = core == 0
            hid[0, m, :, place] = jnp.where(is_low, lo, hi).astype(BF16)
            hid_send[m, :, place] = jnp.where(is_low, hi, lo).astype(BF16)
        hid_hop(m).start()
        return carry

    lax.fori_loop(0, pipe, forward, 0)

    def g_hop(m):
        return remote(gout.at[m], gin.at[m], g_send, g_recv.at[m], section=section - 1)

    def backward(m, carry):
        x, inv, u, scale = normed(m)

        @pl.when((pos < pipe - 1) | (m > 0))
        def _():
            remote(gout.at[m], gin.at[m], g_send, g_recv.at[m], section=beside).wait_recv()

        g = gin[m].astype(F32)
        slope = (g * gate_slope[m]).astype(BF16)
        slopes[0, m] = slope
        back = lax.dot_general(
            slope, wfull[...], (((1,), (1,)), ((), ())), preferred_element_type=F32
        )
        to_pool = jnp.sum(back * u, axis=0, keepdims=True)
        gu = back * scale
        gu = jnp.concatenate(
            [gu[:n_dp, :], gu[text_rows, :] + wide(coef[m]) * to_pool], axis=0
        )
        along = jnp.mean(gu * u, axis=1, keepdims=True)
        gout[m] = (g + inv * (gu - u * along)).astype(BF16)

        @pl.when(pos > 0)
        def _():
            g_hop(m).start()

        slope_hop(m).start()
        return carry

    lax.fori_loop(0, pipe, backward, 0)

    def all_hid():
        return remote(hid_send, hid.at[1], h_sem.at[0], h_sem.at[1], dp=partner)

    def all_slopes():
        return remote(slopes.at[0], slopes.at[1], s_sem.at[0], s_sem.at[1], dp=partner)

    all_hid().wait_recv()
    all_slopes().wait_recv()
    deep = 2 * pipe * rows
    cotangents = slopes[...].reshape(deep, channels)
    for k in range(chips // 2):
        held = hid[:, :, :, 128 * k : 128 * k + 128].reshape(deep, 128)
        both = lax.dot_general(
            held, cotangents, (((0,), (0,)), ((), ())), preferred_element_type=F32
        )
        for j in (0, 1):
            for h in (0, 1):
                at = 64 * j + half * h
                partial[2 * k + j, h] = both[at : at + half, :]

    def r_hop(direction, t, h):
        return remote(
            rs_out.at[direction, t - 1, h],
            rs_in.at[direction, t - 1, h],
            r_send.at[direction, t - 1, h],
            r_recv.at[direction, t - 1, h],
            dp=ahead(direction),
        )

    def r_halves(direction, t):
        return (direction,) if t == 1 else (0, 1)

    for t in range(1, half_ring + 1):
        gap = half_ring - t + 1
        for h in (0, 1):
            for direction in (0, 1):
                if h in r_halves(direction, t):
                    to = lax.rem(chip + (gap if direction == 0 else chips - gap), chips)
                    total = partial[to, h]
                    if t > 1 and h in r_halves(direction, t - 1):
                        r_hop(direction, t - 1, h).wait_recv()
                        total = total + rs_in[direction, t - 2, h].astype(F32)
                    rs_out[direction, t - 1, h] = total.astype(BF16)
                    r_hop(direction, t, h).start()
    for h in (0, 1):
        total = partial[chip, h]
        for direction in (0, 1):
            if half_ring and h in r_halves(direction, half_ring):
                r_hop(direction, half_ring, h).wait_recv()
                total = total + rs_in[direction, half_ring - 1, h].astype(F32)
        out_ref[h * half : (h + 1) * half, :] = total

    for t in range(1, half_ring + 1):
        for h in (0, 1):
            for direction in (0, 1):
                if h in halves(direction, t):
                    w_hop(direction, t, h).wait_send()
                    w_share(direction, t, h).wait_send()
                if h in r_halves(direction, t):
                    r_hop(direction, t, h).wait_send()
    w_own().wait_send()
    routed.wait_send()
    all_hid().wait_send()
    all_slopes().wait_send()

    @pl.when(pos < pipe - 1)
    def _():
        top_feed(0).wait_send()
        remote(xout, xin, x_send, x_recv.at[0], section=beside).wait_send()

    @pl.when(pos > 0)
    def _():
        row_feed(0).wait_send()
        remote(gout, gin, g_send, g_recv.at[0], section=beside).wait_send()


def local(pipe, n_dp, lat_raw, txt_raw, lat_embed, txt_embed, image_owner, text_len, weights, top_grad):
    channels = txt_embed.shape[1]
    rows = 2 * n_dp
    chips = n_dp // 2
    steps = max(chips // 2, 1)
    share = channels // n_dp
    vmem = pl.BlockSpec(memory_space=pltpu.VMEM)
    dma = pltpu.SemaphoreType.DMA
    out = pl.pallas_call(
        functools.partial(step_kernel, n_dp, pipe),
        out_shape=jax.ShapeDtypeStruct((share, channels), F32),
        in_specs=[vmem] * 5 + [pl.BlockSpec(memory_space=pl.ANY)] + [vmem] * 2,
        out_specs=vmem,
        scratch_shapes=[
            pltpu.VMEM(txt_embed.shape, BF16),
            pltpu.VMEM((channels, channels), BF16),
            pltpu.VMEM((n_dp, 2, channels), F32),
            pltpu.VMEM((n_dp, 2, channels), F32),
            pltpu.VMEM((rows, channels), F32),
            pltpu.VMEM((rows, channels), BF16),
            pltpu.VMEM((pipe, n_dp, 128), F32),
            pltpu.VMEM((pipe, rows, channels), BF16),
            pltpu.VMEM((pipe, rows, channels), BF16),
            pltpu.VMEM((pipe, rows, channels), BF16),
            pltpu.VMEM((pipe, rows, channels), BF16),
            pltpu.VMEM((pipe, rows, channels), F32),
            pltpu.VMEM((pipe, rows, channels // 2), BF16),
            pltpu.VMEM((2, pipe, rows, channels // 2), BF16),
            pltpu.VMEM((2, pipe, rows, channels), BF16),
            pltpu.VMEM((chips, 2, share // 2, channels), F32),
            pltpu.VMEM((2, steps, 2, share // 2, channels), BF16),
            pltpu.VMEM((2, steps, 2, share // 2, channels), BF16),
            dma((EMB_CHUNKS,)),
            dma((2,)),
            dma((2, steps, 2)),
            dma((2, steps, 2)),
            dma((2, steps + 1, 2)),
            dma((2, steps + 1, 2)),
            dma((2,)),
            dma(()),
            dma((pipe,)),
            dma(()),
            dma((pipe,)),
            dma((2,)),
            dma((2,)),
            dma((2, steps, 2)),
            dma((2, steps, 2)),
        ],
        compiler_params=pltpu.CompilerParams(
            collective_id=0, has_side_effects=True, vmem_limit_bytes=48 * 1024 * 1024
        ),
        name="step",
    )(
        image_owner,
        text_len,
        lat_raw.reshape(n_dp, lat_raw.shape[-1]),
        txt_raw.reshape(n_dp, txt_raw.shape[-1]),
        lat_embed,
        txt_embed,
        weights[0],
        top_grad[0, 0],
    )
    return out[None]


def solution(mesh, pipe=8):
    placed = (
        P("section", None, "dp", None),
        P("section", None, "dp", None),
        P(),
        P(),
        P(),
        P(),
        P("section", "dp", None),
        P("dp", "section", None, None),
    )
    return jax.shard_map(
        functools.partial(local, pipe, mesh.shape["dp"]),
        mesh=mesh,
        in_specs=placed,
        out_specs=P("section", "dp", None),
        check_vma=False,
    )
```

time: 697 us -> 139 us (0.20)
  starting transfers between devices: 260 us -> 0 us
  waiting for transfers between devices: 242 us -> 0 us
  Pallas kernels: 0 us -> 132 us
  matrix products: 65.9 us -> 0 us
  other arithmetic: 61.5 us -> 0 us
  loops' own time: 22.6 us -> 0 us
  local copies, waits for them, and re-layouts: 26.1 us -> 6.35 us
  between operations: 13.5 us -> 0.02 us
    ppermute x56 -> x0, starting transfers between devices: 243 us -> none  [the longest x28 207 us: extended(): lax.ppermute(tail, axis, [(i, (i + 1) % count) for i in range(ends)])]
    pallas_call x0 -> x1, Pallas kernels: none -> 132 us  [local(): pl.pallas_call(functools.partial(step_kernel, n_dp, pipe), out_shape=jax....]
    ppermute x56 -> x0, waiting for transfers between devices: 117 us -> none  [the longest x28 94 us: extended(): lax.ppermute(head, axis, [((i + 1) % count, i) for i in range(ends)])]
    reduce_scatter x1 -> x0, waiting for transfers between devices: 100 us -> none  [local(): lax.psum_scatter(lax.dot_general(flat_hidden, flat_slope, (((0,), (0,)),...]
    dot_general x27 -> x0, matrix products: 65.9 us -> none  [the longest x8 22.4 us: backward(): jnp.dot(hidden_layer_state, weight_fwd, preferred_element_type=jnp.float32)]
    reduce_sum x40 -> x0, other arithmetic: 26.4 us -> none  [the longest x16 9.84 us: modulate(): jnp.mean(tokens_in * tokens_in, axis=1, keepdims=True) + norm_eps]
    another operation x32 -> x0, loops' own time: 22.6 us -> none  [the longest x15 10.7 us: retreat(): return lax.cond(active, retreat_do_work, retreat_no_work, saved_rows)]
    all_to_all x2 -> x0, starting transfers between devices: 17.4 us -> none  [the longest x1 13.8 us: local(): lax.all_to_all(jnp.take(text_rows, dest_order, axis=0), 'dp', split_axis=...]
  transfers between devices with their start and end apart: 60 -> 0, of which waited for: 32 -> 0; matrix products, arithmetic and copies ran while one was open for 2% -> 0% of each run, Pallas kernels for 0% -> 0%
where the time goes in v1:
time: 139 us
  Pallas kernels  132 us (95%)
  local copies, waits for them, and re-layouts  6.35 us (5%)
    pallas_call x1, Pallas kernels, local(): pl.pallas_call(functools.partial(step_kernel, n_dp, pipe), out_shape=jax....  132 us
    unnamed x13, local copies, waits for them, and re-layouts  6.35 us

profile of v1, /device:TPU:1, one launch (start us, length us, event | category | flops | bytes accessed | tf_op | source)
XLA Modules:
  0.0 138.6 jit_solution(6258300854190466865)
XLA Ops:
  0.0 0.8 copy.9.owner_ref
  0.8 0.8 copy.10.len_ref
  1.6 0.0 copy-start
  1.6 0.9 copy-done
  2.5 0.0 copy-start.1
  2.5 0.9 copy-done.1
  3.4 0.0 copy-start.2
  3.4 0.8 copy-done.2
  4.2 0.0 copy-start.3
  4.2 0.8 copy-done.3
  5.0 0.0 copy-start.4
  5.0 0.7 copy-done.4
  5.6 132.2 %step.1 = f32[64,1024]{1,0:T(8,128)S(1)} custom-call(s32[48,16]{1,0:T(8,128)S(1)} %copy.9.owner_ref, s32[48,16]{1,0:T(8,128)S(1)} %copy.10.len_ref, bf16[16,16]{1,0:T(8,128)(2,1)S(1)} %bitcast.9, bf16[16,4096]{1,0:T(8,128)(2,1)S(1)} %bitcast.6, bf16[16,1024]{1,0:T(8,128)(2,1)S(1)} %copy-done.3, bf16[4096,1024]{1,0:T(8,128)(2,1)} %emb_hbm.1, ...), custom_call_target="tpu_custom_call" | custom-call | tf_op jit(solution)/shard_map/step/pallas_call | solution.py:433
  137.9 0.7 copy.12
Async XLA Ops:
  1.6 0.9 copy-start
  2.5 0.9 copy-start.1
  3.4 0.8 copy-start.2
  4.2 0.8 copy-start.3
  5.0 0.7 copy-start.4

commit v2 on v1

--- a/solution.py
+++ b/solution.py
@@ -11,22 +11,28 @@
 MESH = pl.DeviceIdType.MESH
 F32 = jnp.float32
 BF16 = jnp.bfloat16
-EMB_CHUNKS = 4
+EMB_CHUNKS = 8
+PARTS = 4
 FWD_CHUNKS = 2
 
 
 def step_kernel(
     n_dp,
     pipe,
+    owner_hbm,
+    len_hbm,
+    lat_hbm,
+    txt_hbm,
+    lat_emb_hbm,
+    emb_hbm,
+    w_hbm,
+    top_hbm,
+    out_ref,
     owner_ref,
     len_ref,
     lat_ref,
     txt_ref,
     lat_emb_ref,
-    emb_hbm,
-    w_ref,
-    top_ref,
-    out_ref,
     emb,
     wfull,
     route_out,
@@ -46,6 +52,7 @@
     rs_out,
     rs_in,
     emb_sem,
+    in_sem,
     route_sem,
     w_send,
     w_recv,
@@ -65,7 +72,7 @@
     half_ring = chips // 2
     channels = wfull.shape[0]
     share = channels // n_dp
-    half = share // 2
+    half = share // PARTS
     rows = 2 * n_dp
     me = lax.axis_index("dp")
     section = lax.axis_index("section")
@@ -93,6 +100,22 @@
         part = pl.ds(i * depth, depth)
         return pltpu.make_async_copy(emb_hbm.at[part], emb.at[part], emb_sem.at[i])
 
+    own_rows = wfull.at[pl.ds(pl.multiple_of(me * share, share), share)]
+    fetches = [
+        pltpu.make_async_copy(src, dst, in_sem.at[i])
+        for i, (src, dst) in enumerate(
+            (
+                (w_hbm, own_rows),
+                (owner_hbm, owner_ref),
+                (len_hbm, len_ref),
+                (lat_hbm, lat_ref),
+                (txt_hbm, txt_ref),
+                (lat_emb_hbm, lat_emb_ref),
+            )
+        )
+    ]
+    for fetch in fetches:
+        fetch.start()
     for i in range(EMB_CHUNKS):
         emb_copy(i).start()
 
@@ -109,19 +132,23 @@
             device_id_type=MESH,
         )
 
-    block = pl.ds(pl.multiple_of(first, pipe), pipe)
-    mine = owner_ref[block, :] == me
+    for fetch in fetches:
+        fetch.wait()
+    columns = owner_ref.shape[1]
+    column = lax.broadcasted_iota(jnp.int32, (1, columns), 1)
     counts = jnp.sum(
-        jnp.where(mine, len_ref[block, :], 0).astype(F32), axis=1, keepdims=True
+        jnp.where(owner_ref[...] == me, len_ref[...], 0).astype(F32), axis=0, keepdims=True
     )
     order = lax.broadcasted_iota(jnp.int32, (n_dp, 128), 0).astype(F32)
     for m in range(pipe):
-        count = jnp.broadcast_to(counts[m : m + 1, :], (n_dp, 128))
+        count = jnp.sum(jnp.where(column == first + m, counts, 0.0), axis=1, keepdims=True)
+        count = jnp.broadcast_to(count, (n_dp, 128))
         coef[m] = jnp.where(order < count, 0.5 / count, 0.0)
-    spot = lax.broadcasted_iota(jnp.int32, (n_dp, n_dp), 0)
-    pick = (spot == owner_ref[pl.ds(section, 1), :]).astype(F32).astype(BF16)
-
-    wfull[pl.ds(pl.multiple_of(me * share, share), share), :] = w_ref[...]
+    owners = jnp.sum(
+        jnp.where(column == section, owner_ref[...], 0).astype(F32), axis=1, keepdims=True
+    )
+    spot = lax.broadcasted_iota(jnp.int32, (n_dp, n_dp), 1).astype(F32)
+    pick = (spot == owners).astype(F32).astype(BF16)
     pl.semaphore_wait(barrier, n_dp - 1 + pipe - 1)
 
     def w_block(owner_chip, whose, h):
@@ -136,16 +163,18 @@
         step = 1 if direction == 0 else chips - 1
         return lax.rem(chip + step, chips) * 2 + core
 
+    every = tuple(range(PARTS))
+
+    def side(direction):
+        return every[: PARTS // 2] if direction == 0 else every[PARTS // 2 :]
+
     def halves(direction, t):
-        if t == half_ring:
-            return (direction,)
-        return (0, 1)
+        return side(direction) if t == half_ring else every
 
     def w_hop(direction, t, h):
-        src = w_ref.at[pl.ds(h * half, half)] if t == 1 else w_block(origin(direction, t - 1), core, h)
-        dst = w_block(origin(direction, t - 1) if t > 1 else chip, core, h)
+        blk = w_block(origin(direction, t - 1) if t > 1 else chip, core, h)
         return remote(
-            src, dst, w_send.at[direction, t - 1, h], w_recv.at[direction, t - 1, h], dp=ahead(direction)
+            blk, blk, w_send.at[direction, t - 1, h], w_recv.at[direction, t - 1, h], dp=ahead(direction)
         )
 
     def w_land(direction, t, h):
@@ -163,22 +192,21 @@
         return remote(blk, blk, pw_send.at[direction, t, h], pw_recv.at[direction, t, h], dp=partner)
 
     def w_own():
-        blk = wfull.at[pl.ds(pl.multiple_of(me * share, share), share)]
-        return remote(w_ref, blk, pw_send.at[0, 0, 0], pw_recv.at[0, 0, 0], dp=partner)
+        return remote(own_rows, own_rows, pw_send.at[0, 0, 0], pw_recv.at[0, 0, 0], dp=partner)
 
     def w_owned():
         blk = wfull.at[pl.ds(pl.multiple_of(partner * share, share), share)]
-        return remote(w_ref, blk, pw_send.at[0, 0, 0], pw_recv.at[0, 0, 0], dp=partner)
+        return remote(blk, blk, pw_send.at[0, 0, 0], pw_recv.at[0, 0, 0], dp=partner)
 
     if half_ring:
-        for h in (0, 1):
+        for h in range(PARTS):
             for direction in (0, 1):
                 if h in halves(direction, 1):
                     w_hop(direction, 1, h).start()
     w_own().start()
 
     def top_feed(slot):
-        return remote(top_ref, gin.at[slot], feed_sem.at[0], g_recv.at[slot], section=last)
+        return remote(top_hbm, gin.at[slot], feed_sem.at[0], g_recv.at[slot], section=last)
 
     @pl.when(pos < pipe - 1)
     def _():
@@ -186,7 +214,7 @@
 
     @pl.when(pos == pipe - 1)
     def _():
-        gin[0] = top_ref[...]
+        pltpu.make_async_copy(top_hbm, gin.at[0], g_recv.at[0]).start()
 
     def encode(i, so_far):
         emb_copy(i).wait()
@@ -194,7 +222,7 @@
         return so_far + jnp.dot(txt_ref[:, part], emb[part, :], preferred_element_type=F32)
 
     def ring_step(t):
-        for h in (0, 1):
+        for h in range(PARTS):
             for direction in (0, 1):
                 if h in halves(direction, t):
                     w_land(direction, t, h).wait_recv()
@@ -206,8 +234,9 @@
     for i in range(EMB_CHUNKS):
         text = encode(i, text)
     lat = jnp.dot(lat_ref[...], lat_emb_ref[...], preferred_element_type=F32)
-    lat_sel = jnp.dot(pick, lat.astype(BF16), preferred_element_type=F32)
-    text_sel = jnp.dot(pick, text.astype(BF16), preferred_element_type=F32)
+    over_rows = (((0,), (0,)), ((), ()))
+    lat_sel = lax.dot_general(pick, lat.astype(BF16), over_rows, preferred_element_type=F32)
+    text_sel = lax.dot_general(pick, text.astype(BF16), over_rows, preferred_element_type=F32)
     for i in range(n_dp):
         route_out[i, 0:1, :] = lat_sel[i : i + 1, :]
         route_out[i, 1:2, :] = text_sel[i : i + 1, :]
@@ -247,7 +276,7 @@
         ring_step(t)
     w_owned().wait_recv()
     for t in range(1, half_ring + 1):
-        for h in (0, 1):
+        for h in range(PARTS):
             for direction in (0, 1):
                 if h in halves(direction, t):
                     w_shared(direction, t, h).wait_recv()
@@ -280,7 +309,7 @@
     def slope_hop(m):
         return remote(slopes.at[0, m], slopes.at[1, m], s_sem.at[0], s_sem.at[1], dp=partner)
 
-    def forward(m, carry):
+    def forward(m):
         @pl.when((pos > 0) | (m > 0))
         def _():
             remote(xout.at[m], xin.at[m], x_send, x_recv.at[m], section=beside).wait_recv()
@@ -309,42 +338,47 @@
             hid[0, m, :, place] = jnp.where(is_low, lo, hi).astype(BF16)
             hid_send[m, :, place] = jnp.where(is_low, hi, lo).astype(BF16)
         hid_hop(m).start()
-        return carry
-
-    lax.fori_loop(0, pipe, forward, 0)
 
     def g_hop(m):
         return remote(gout.at[m], gin.at[m], g_send, g_recv.at[m], section=section - 1)
 
-    def backward(m, carry):
+    def backward(m):
         x, inv, u, scale = normed(m)
 
-        @pl.when((pos < pipe - 1) | (m > 0))
-        def _():
-            remote(gout.at[m], gin.at[m], g_send, g_recv.at[m], section=beside).wait_recv()
-
+        remote(gout.at[m], gin.at[m], g_send, g_recv.at[m], section=beside).wait_recv()
         g = gin[m].astype(F32)
         slope = (g * gate_slope[m]).astype(BF16)
         slopes[0, m] = slope
-        back = lax.dot_general(
-            slope, wfull[...], (((1,), (1,)), ((), ())), preferred_element_type=F32
-        )
-        to_pool = jnp.sum(back * u, axis=0, keepdims=True)
-        gu = back * scale
-        gu = jnp.concatenate(
-            [gu[:n_dp, :], gu[text_rows, :] + wide(coef[m]) * to_pool], axis=0
-        )
-        along = jnp.mean(gu * u, axis=1, keepdims=True)
-        gout[m] = (g + inv * (gu - u * along)).astype(BF16)
+        slope_hop(m).start()
 
         @pl.when(pos > 0)
         def _():
+            back = lax.dot_general(
+                slope, wfull[...], (((1,), (1,)), ((), ())), preferred_element_type=F32
+            )
+            to_pool = jnp.sum(back * u, axis=0, keepdims=True)
+            gu = back * scale
+            gu = jnp.concatenate(
+                [gu[:n_dp, :], gu[text_rows, :] + wide(coef[m]) * to_pool], axis=0
+            )
+            along = jnp.mean(gu * u, axis=1, keepdims=True)
+            gout[m] = (g + inv * (gu - u * along)).astype(BF16)
             g_hop(m).start()
 
-        slope_hop(m).start()
+    lag = jnp.where(pos == pipe - 1, 0, jnp.where(pos == pipe - 2, max(pipe - 2, 0), pipe - 1))
+
+    def turn(t, carry):
+        @pl.when(t < pipe)
+        def _():
+            forward(t)
+
+        @pl.when((t >= lag) & (t < lag + pipe))
+        def _():
+            backward(t - lag)
+
         return carry
 
-    lax.fori_loop(0, pipe, backward, 0)
+    lax.fori_loop(0, 2 * pipe - 1, turn, 0)
 
     def all_hid():
         return remote(hid_send, hid.at[1], h_sem.at[0], h_sem.at[1], dp=partner)
@@ -362,7 +396,7 @@
             held, cotangents, (((0,), (0,)), ((), ())), preferred_element_type=F32
         )
         for j in (0, 1):
-            for h in (0, 1):
+            for h in range(PARTS):
                 at = 64 * j + half * h
                 partial[2 * k + j, h] = both[at : at + half, :]
 
@@ -376,11 +410,11 @@
         )
 
     def r_halves(direction, t):
-        return (direction,) if t == 1 else (0, 1)
+        return side(direction) if t == 1 else every
 
     for t in range(1, half_ring + 1):
         gap = half_ring - t + 1
-        for h in (0, 1):
+        for h in range(PARTS):
             for direction in (0, 1):
                 if h in r_halves(direction, t):
                     to = lax.rem(chip + (gap if direction == 0 else chips - gap), chips)
@@ -390,7 +424,7 @@
                         total = total + rs_in[direction, t - 2, h].astype(F32)
                     rs_out[direction, t - 1, h] = total.astype(BF16)
                     r_hop(direction, t, h).start()
-    for h in (0, 1):
+    for h in range(PARTS):
         total = partial[chip, h]
         for direction in (0, 1):
             if half_ring and h in r_halves(direction, half_ring):
@@ -399,7 +433,7 @@
         out_ref[h * half : (h + 1) * half, :] = total
 
     for t in range(1, half_ring + 1):
-        for h in (0, 1):
+        for h in range(PARTS):
             for direction in (0, 1):
                 if h in halves(direction, t):
                     w_hop(direction, t, h).wait_send()
@@ -413,7 +447,7 @@
 
     @pl.when(pos < pipe - 1)
     def _():
-        top_feed(0).wait_send()
+        top_feed(1).wait_send()
         remote(xout, xin, x_send, x_recv.at[0], section=beside).wait_send()
 
     @pl.when(pos > 0)
@@ -433,9 +467,14 @@
     out = pl.pallas_call(
         functools.partial(step_kernel, n_dp, pipe),
         out_shape=jax.ShapeDtypeStruct((share, channels), F32),
-        in_specs=[vmem] * 5 + [pl.BlockSpec(memory_space=pl.ANY)] + [vmem] * 2,
+        in_specs=[pl.BlockSpec(memory_space=pl.ANY)] * 8,
         out_specs=vmem,
         scratch_shapes=[
+            pltpu.VMEM(image_owner.shape[::-1], jnp.int32),
+            pltpu.VMEM(image_owner.shape[::-1], jnp.int32),
+            pltpu.VMEM((n_dp, lat_raw.shape[-1]), BF16),
+            pltpu.VMEM((n_dp, txt_raw.shape[-1]), BF16),
+            pltpu.VMEM(lat_embed.shape, BF16),
             pltpu.VMEM(txt_embed.shape, BF16),
             pltpu.VMEM((channels, channels), BF16),
             pltpu.VMEM((n_dp, 2, channels), F32),
@@ -451,15 +490,16 @@
             pltpu.VMEM((pipe, rows, channels // 2), BF16),
             pltpu.VMEM((2, pipe, rows, channels // 2), BF16),
             pltpu.VMEM((2, pipe, rows, channels), BF16),
-            pltpu.VMEM((chips, 2, share // 2, channels), F32),
-            pltpu.VMEM((2, steps, 2, share // 2, channels), BF16),
-            pltpu.VMEM((2, steps, 2, share // 2, channels), BF16),
+            pltpu.VMEM((chips, PARTS, share // PARTS, channels), F32),
+            pltpu.VMEM((2, steps, PARTS, share // PARTS, channels), BF16),
+            pltpu.VMEM((2, steps, PARTS, share // PARTS, channels), BF16),
             dma((EMB_CHUNKS,)),
+            dma((6,)),
             dma((2,)),
-            dma((2, steps, 2)),
-            dma((2, steps, 2)),
-            dma((2, steps + 1, 2)),
-            dma((2, steps + 1, 2)),
+            dma((2, steps, PARTS)),
+            dma((2, steps, PARTS)),
+            dma((2, steps + 1, PARTS)),
+            dma((2, steps + 1, PARTS)),
             dma((2,)),
             dma(()),
             dma((pipe,)),
@@ -467,16 +507,16 @@
             dma((pipe,)),
             dma((2,)),
             dma((2,)),
-            dma((2, steps, 2)),
-            dma((2, steps, 2)),
+            dma((2, steps, PARTS)),
+            dma((2, steps, PARTS)),
         ],
         compiler_params=pltpu.CompilerParams(
-            collective_id=0, has_side_effects=True, vmem_limit_bytes=48 * 1024 * 1024
+            collective_id=0, has_side_effects=True, vmem_limit_bytes=60 * 1024 * 1024
         ),
         name="step",
     )(
-        image_owner,
-        text_len,
+        image_owner.T,
+        text_len.T,
         lat_raw.reshape(n_dp, lat_raw.shape[-1]),
         txt_raw.reshape(n_dp, txt_raw.shape[-1]),
         lat_embed,

time: 139 us -> 128 us (0.921)
  Pallas kernels: 132 us -> 126 us
  local copies, waits for them, and re-layouts: 6.35 us -> 1.67 us
    pallas_call x1, Pallas kernels: 132 us -> 126 us  [local(): pl.pallas_call(functools.partial(step_kernel, n_dp, pipe), out_shape=jax....]
    unnamed x13 -> x1, local copies, waits for them, and re-layouts: 6.35 us -> 1.67 us
where the time goes in v2:
time: 128 us
  Pallas kernels  126 us (98%)
  local copies, waits for them, and re-layouts  1.67 us (1%)
    pallas_call x1, Pallas kernels, local(): pl.pallas_call(functools.partial(step_kernel, n_dp, pipe), out_shape=jax....  126 us

profile of v2, /device:TPU:1, one launch (start us, length us, event | category | flops | bytes accessed | tf_op | source)
XLA Modules:
  0.0 128.1 jit_solution(2042159994454028355)
XLA Ops:
  0.0 126.4 %step.1 = f32[64,1024]{1,0:T(8,128)} custom-call(s32[16,48]{1,0:T(8,128)} %bitcast.11, s32[16,48]{1,0:T(8,128)} %bitcast.12, bf16[16,16]{1,0:T(8,128)(2,1)} %bitcast.13, bf16[16,4096]{1,0:T(8,128)(2,1)} %bitcast.8, bf16[16,1024]{1,0:T(8,128)(2,1)} %lat_emb_hbm.1, bf16[4096,1024]{1,0:T(8,128)(2,1)} %emb_hbm.1, bf16[64,1024]{1,0:T(8,128)(2,1)} %bitcast.9, ...), custom_call_target="tpu_custom_call" | custom-call | tf_op jit(solution)/shard_map/step/pallas_call | solution.py:467
  126.4 1.7 %copy.10 = f32[1,64,1024]{2,1,0:T(8,128)} copy(f32[1,64,1024]{2,1,0:T(8,128)} %bitcast.7) | data formatting | bytes 524288
